TPU v7x, 256 devices: a whole 4x4x8 slice. The times are simulated.
256 devices in a mesh: band: 8 (over y, core), plane: 32 (over x, z).
Axes of the slice: x: 4, y: 4, z: 8, core: 2. Of those that a mesh axis runs over, the one named last changes fastest.
Arguments:
- psi: float32 [2, 8, 4096, 128], P(None, 'band', 'plane'), may hold values from -8 to 8
- potential: float32 [96, 9216], P('plane'), may hold values from 0 to 2
- stick_column: int32 [4096], P('plane'), may hold values from 0 to 9215, as said below
- stick_length: int32 [4096], P('plane'), may hold values from 0 to 49, as said below
Outputs:
- psi_new: float32 [2, 8, 4096, 128], P(None, 'band', 'plane')
- potential_new: float32 [96, 9216], P('plane')
Inputs may be any that keep to these rules, and one draw needn't show every extreme that they name: `stick_column`: within each device's block of 128 slots the live sticks come first and the other slots are empty with column 0. Over all devices the live slots hold every column (mx mod 96) * 96 + (my mod 96) with mx * mx + my * my <= 576 exactly once, in an order drawn from the seed; some device's block is full and the others hold fewer. `stick_length`: A live slot's length is 2 h + 1, with h the largest whole number such that mx * mx + my * my + h * h <= 576 for its column; empty slots have length 0.
All inputs are finite; a program needn't handle non-finite values.
Results may differ from a plain program's by a relative error of at most 0.0001.
Values sent between devices are 32-bit elements; how exact they have to be, the bound alone decides.
No kernel may reach another device: no remote copies, remote signals or barrier semaphores. Data moves between devices by JAX's collectives and lax.ppermute only.
A program may use at most 64 MiB of HBM per device.

v0:
```python
import math
import jax
import jax.numpy as jnp
from jax import lax
from jax.sharding import PartitionSpec as P

NG = 96
RAD = 24
STICK_COEFFS = 128
BAND_DEV = 1
HIGHEST = lax.Precision.HIGHEST
TIMESTEP = 0.6
LINEAR_GAIN = 0.5
CUBIC_GAIN = 0.3


def turning(values):
    return values.astype(jnp.float32) * (2.0 * math.pi / NG)


def height_tables(lengths, columns, planes, device_list):
    order = jnp.arange(STICK_COEFFS, dtype=jnp.int32)
    height = (
        jnp.arange(device_list, dtype=jnp.int32)[None, :] * planes
        + jnp.arange(planes, dtype=jnp.int32)[:, None]
    )
    scale = NG ** (-0.5)
    wave_angle = turning(order[:, None, None] * height[None, :, :] % NG)
    wave = (jnp.cos(wave_angle) * scale, jnp.sin(wave_angle) * scale)
    half = (lengths - 1) // 2
    shift_angle = -turning(height[:, :, None] * half[None, None, :] % NG)
    shift = (jnp.cos(shift_angle), jnp.sin(shift_angle))
    mask = (order[None, :] < lengths[:, None]).astype(jnp.float32)
    first = columns // NG
    second = columns % NG
    first = jnp.where(first > NG // 2, first - NG, first)
    second = jnp.where(second > NG // 2, second - NG, second)
    depth = order[None, :] - half[:, None]
    kinetic = (
        ((first * first + second * second)[:, None] + depth * depth).astype(jnp.float32)
        / (RAD * RAD)
        * mask
    )
    return (wave, shift, mask, kinetic)


def along_height(terms, tables):
    wave, shift = (tables[0], tables[1])

    def contract(left, right):
        return jnp.einsum("bsj,jdn->bdns", left, right, precision=HIGHEST)

    upper_real = contract(terms[0], wave[0]) - contract(terms[1], wave[1])
    upper_imag = contract(terms[0], wave[1]) + contract(terms[1], wave[0])
    return jnp.stack(
        [
            upper_real * shift[0] - upper_imag * shift[1],
            upper_real * shift[1] + upper_imag * shift[0],
        ]
    )


def from_height(values, tables):
    wave, shift, mask = (tables[0], tables[1], tables[2])
    turned_real = values[0] * shift[0] + values[1] * shift[1]
    turned_imag = values[1] * shift[0] - values[0] * shift[1]

    def contract(left, right):
        return jnp.einsum("bdns,jdn->bsj", left, right, precision=HIGHEST)

    real_part = contract(turned_real, wave[0]) + contract(turned_imag, wave[1])
    imag_part = contract(turned_imag, wave[0]) - contract(turned_real, wave[1])
    return jnp.stack([real_part * mask, imag_part * mask])


def plane_tables():
    index = jnp.arange(NG, dtype=jnp.int32)
    angle = turning(index[:, None] * index[None, :] % NG)
    scale = NG ** (-0.5)
    return (jnp.cos(angle) * scale, jnp.sin(angle) * scale)


def plane_transform(values, cosine, sine):
    bands, planes = (values.shape[1], values.shape[2])
    real_part = values[0].reshape(bands, planes, NG, NG)
    imag_part = values[1].reshape(bands, planes, NG, NG)

    def inner(left, right):
        return jnp.einsum("bdmk,ky->bdmy", left, right, precision=HIGHEST)

    def outer(left, right):
        return jnp.einsum("mx,bdmy->bdxy", left, right, precision=HIGHEST)

    middle_real = inner(real_part, cosine) - inner(imag_part, sine)
    middle_imag = inner(real_part, sine) + inner(imag_part, cosine)
    final_real = outer(cosine, middle_real) - outer(sine, middle_imag)
    final_imag = outer(sine, middle_real) + outer(cosine, middle_imag)
    return jnp.stack([final_real, final_imag]).reshape(2, bands, planes, NG * NG)


def cell_slots(columns, lengths):
    count = columns.shape[0]
    target = jnp.where(lengths > 0, columns, NG * NG)
    table = jnp.full((NG * NG,), -1, jnp.int32)
    return table.at[target].set(jnp.arange(count, dtype=jnp.int32), mode="drop")


def spread_columns(values, table):
    picked = jnp.take(values, jnp.maximum(table, 0), axis=3)
    return jnp.where(table >= 0, picked, 0.0)


def modulus(field):
    return jnp.sum(field[0] * field[0] + field[1] * field[1], axis=0)


def advance(applied, power):
    factor = TIMESTEP / power
    return jnp.stack([factor * applied[1], -factor * applied[0]])


def shards(psi, potential, stick_column, stick_length):
    device_list = lax.axis_size("plane")
    planes = potential.shape[0]
    slots = stick_column.shape[0]
    bands = psi.shape[1]
    cosine, sine = plane_tables()
    own = height_tables(stick_length, stick_column, planes, device_list)
    term = psi * own[2]
    columns, lengths = (
        lax.all_gather(stick_column, "plane", axis=0, tiled=True),
        lax.all_gather(stick_length, "plane", axis=0, tiled=True),
    )
    given_cells = cell_slots(columns, lengths)
    total = term
    before = jnp.zeros((planes, NG * NG), jnp.float32)
    for power in range(1, 4):
        arrived = lax.all_to_all(
            along_height(term, own), "plane", split_axis=3, concat_axis=3, tiled=True
        ).reshape(2, bands, planes, device_list * slots)
        field = plane_transform(spread_columns(arrived, given_cells), cosine, sine)
        if power == 1:
            before = modulus(field)
        spectrum = plane_transform(field * potential, cosine, -sine)
        picked = spectrum[:, :, :, columns].reshape(2, bands, planes, device_list, slots)
        returned = lax.all_to_all(picked, "plane", split_axis=3, concat_axis=3, tiled=True)
        term = advance(from_height(returned, own) + own[3] * term, power)
        total = total + term
    arrived = lax.all_to_all(
        along_height(total, own), "plane", split_axis=3, concat_axis=3, tiled=True
    ).reshape(2, bands, planes, device_list * slots)
    after = modulus(plane_transform(spread_columns(arrived, given_cells), cosine, sine))
    change = (after - before) / BAND_DEV
    whole = lax.psum(change, "band")
    potential_new = potential + LINEAR_GAIN * whole + CUBIC_GAIN * whole * whole * whole
    return (total, potential_new)


def solution(mesh):
    in_specs = (P(None, "band", "plane", None), P("plane", None), P("plane"), P("plane"))
    out_specs = (P(None, "band", "plane", None), P("plane", None))
    return jax.shard_map(shards, mesh=mesh, in_specs=in_specs, out_specs=out_specs, check_vma=False)
```

profile of v0, /device:TPU:2, one launch (start us, length us, event | category | flops | bytes accessed | tf_op | source)
XLA Modules:
  0.0 968.3 jit_solution(16766717710354045417)
XLA Ops:
  12.2 11.6 %all-to-all-start = ((f32[2,1,3,32,128]{4,0,2,1,3:T(2,128)}), f32[2,1,3,32,128]{4,0,2,1,3:T(2,128)S(1)}, u32[]{:S(2)}, u32[]{:S(2)}) async-start(f32[2,1,3,32,128]{4,0,2,1,3:T(2,128)} %copy.177), calls=%async_computation | async-start | bytes 196608 | tf_op jit(solution)/shard_map/all_to_all | solution.py:138
  23.8 39.6 %all-gather = s32[32,1,128]{2,1,0:T(1,128)S(1)} all-gather(s32[1,1,128]{2,1,0:T(1,128)} %bitcast.566), channel_id=1, replica_groups=mesh['band'=8,'plane'=32] {'plane'}, dimensions={0}, use_global_device_ids=true | all-gather | bytes 16896 | tf_op jit(solution)/shard_map/all_gather | solution.py:132
  63.4 36.7 %all-gather.1 = s32[32,1,128]{2,1,0:T(1,128)S(1)} all-gather(s32[1,1,128]{2,1,0:T(1,128)} %bitcast.567), channel_id=1, replica_groups=mesh['band'=8,'plane'=32] {'plane'}, dimensions={0}, use_global_device_ids=true | all-gather | bytes 16896 | tf_op jit(solution)/shard_map/all_gather | solution.py:131
  100.1 15.5 %scatter_custom_fusion = s32[9216]{0:T(1024)S(1)} fusion(s32[4096]{0:T(1024)S(1)} %get-tuple-element.40, s32[4096]{0:T(1024)S(1)} %iota.105, s32[]{:T(128)} %constant.56.clone.1), kind=kCustom, calls=%fused_computation.291 | custom fusion | bytes 36868 | tf_op jit(solution)/shard_map/scatter | solution.py:105
  116.4 4.3 copy.179
  120.7 65.0 %gather_fusion.3 = f32[9216,2,3]{2,1,0:T(2,128)} fusion(f32[2,3,4096]{1,0,2:T(2,128)} %bitcast.554, s32[9216]{0:T(1024)S(1)} %maximum_clamp_fusion), kind=kCustom, calls=%fused_computation.clone | custom fusion | bytes 479232 | tf_op jit(solution)/shard_map/jit(_take)/gather | solution.py:109
  185.7 42.6 %fusion.3 = f32[2,1,3,9216]{2,0,3,1:T(2,128)S(1)} fusion(f32[9216,2,3]{2,1,0:T(2,128)} %gather_fusion.3, pred[9216]{0:T(1024)(128)(4,1)S(1)} %get-tuple-element.38, pred[9216]{0:T(1024)(128)(4,1)S(1)} %get-tuple-element.37), kind=kLoop, calls=%fused_computation.15 | loop fusion | flops 110592 | bytes 460800 | tf_op jit(solution)/shard_map/jit(_where)/select_n | solution.py:110
  228.3 8.5 fusion.517
  236.8 3.1 copy.281
  240.9 3.6 copy.282
  254.3 8.9 copy.194
  263.2 31.8 %gather_fusion = f32[4096,2,3]{2,1,0:T(2,128)} fusion(f32[2,3,9216]{1,0,2:T(2,128)} %bitcast.550, s32[4096]{0:T(1024)S(1)} %get-tuple-element.39), kind=kCustom, calls=%fused_computation.4 | custom fusion | bytes 212992 | tf_op jit(solution)/shard_map/gather | solution.py:145
  295.1 5.8 copy.196
  300.9 6.5 all-to-all-start.1
  307.5 8.7 all-to-all-done.1
  321.1 13.5 %all_to_all.35 = f32[2,1,3,32,128]{4,0,2,1,3:T(2,128)S(1)} all-to-all(f32[2,1,3,32,128]{4,0,2,1,3:T(2,128)S(1)} %copy.199), channel_id=1, replica_groups=mesh['band'=8,'plane'=32] {'plane'}, dimensions={3} | all-to-all | bytes 196608 | tf_op jit(solution)/shard_map/all_to_all | solution.py:138
  334.6 4.3 copy.201
  339.0 65.0 %gather_fusion.4 = f32[9216,2,3]{2,1,0:T(2,128)} fusion(f32[2,3,4096]{1,0,2:T(2,128)} %bitcast.555, s32[9216]{0:T(1024)S(1)} %maximum_clamp_fusion), kind=kCustom, calls=%fused_computation.1.clone | custom fusion | bytes 479232 | tf_op jit(solution)/shard_map/jit(_take)/gather | solution.py:109
  403.9 42.6 %fusion.2 = f32[2,1,3,9216]{2,0,3,1:T(2,128)S(1)} fusion(f32[9216,2,3]{2,1,0:T(2,128)} %gather_fusion.4, pred[9216]{0:T(1024)(128)(4,1)S(1)} %get-tuple-element.38, pred[9216]{0:T(1024)(128)(4,1)S(1)} %get-tuple-element.37), kind=kLoop, calls=%fused_computation.13 | loop fusion | flops 110592 | bytes 460800 | tf_op jit(solution)/shard_map/jit(_where)/select_n | solution.py:110
  446.5 8.5 fusion.516
  455.0 3.1 copy.285
  459.1 3.3 copy.286
  472.2 8.9 copy.216
  481.1 31.8 %gather_fusion.1 = f32[4096,2,3]{2,1,0:T(2,128)} fusion(f32[2,3,9216]{1,0,2:T(2,128)} %bitcast.552, s32[4096]{0:T(1024)S(1)} %get-tuple-element.39), kind=kCustom, calls=%fused_computation.5 | custom fusion | bytes 212992 | tf_op jit(solution)/shard_map/gather | solution.py:145
  513.0 5.8 copy.218
  518.8 5.5 all-to-all-start.3
  524.3 8.9 all-to-all-done.3
  538.1 13.5 %all_to_all.36 = f32[2,1,3,32,128]{4,0,2,1,3:T(2,128)S(1)} all-to-all(f32[2,1,3,32,128]{4,0,2,1,3:T(2,128)S(1)} %copy.221), channel_id=1, replica_groups=mesh['band'=8,'plane'=32] {'plane'}, dimensions={3} | all-to-all | bytes 196608 | tf_op jit(solution)/shard_map/all_to_all | solution.py:138
  551.6 4.3 copy.223
  556.0 65.0 %gather_fusion.5 = f32[9216,2,3]{2,1,0:T(2,128)} fusion(f32[2,3,4096]{1,0,2:T(2,128)} %bitcast.556, s32[9216]{0:T(1024)S(1)} %maximum_clamp_fusion), kind=kCustom, calls=%fused_computation.2.clone | custom fusion | bytes 479232 | tf_op jit(solution)/shard_map/jit(_take)/gather | solution.py:109
  620.9 42.6 %fusion.1 = f32[2,1,3,9216]{2,0,3,1:T(2,128)S(1)} fusion(f32[9216,2,3]{2,1,0:T(2,128)} %gather_fusion.5, pred[9216]{0:T(1024)(128)(4,1)S(1)} %get-tuple-element.38, pred[9216]{0:T(1024)(128)(4,1)S(1)} %get-tuple-element.37), kind=kLoop, calls=%fused_computation.11 | loop fusion | flops 110592 | bytes 460800 | tf_op jit(solution)/shard_map/jit(_where)/select_n | solution.py:110
  663.5 8.5 fusion.515
  672.0 3.1 copy.289
  676.1 3.3 copy.290
  689.2 8.9 copy.238
  698.1 31.8 %gather_fusion.2 = f32[4096,2,3]{2,1,0:T(2,128)} fusion(f32[2,3,9216]{1,0,2:T(2,128)} %bitcast.551, s32[4096]{0:T(1024)S(1)} %get-tuple-element.39), kind=kCustom, calls=%fused_computation.6 | custom fusion | bytes 212992 | tf_op jit(solution)/shard_map/gather | solution.py:145
  729.9 5.8 copy.240
  735.8 5.0 all-to-all-start.5
  741.0 8.8 all-to-all-done.5
  754.8 13.5 %all_to_all.37 = f32[2,1,3,32,128]{4,0,2,1,3:T(2,128)S(1)} all-to-all(f32[2,1,3,32,128]{4,0,2,1,3:T(2,128)S(1)} %copy.243), channel_id=1, replica_groups=mesh['band'=8,'plane'=32] {'plane'}, dimensions={3} | all-to-all | bytes 196608 | tf_op jit(solution)/shard_map/all_to_all | solution.py:149
  768.3 4.3 copy.245
  772.6 65.0 %gather_fusion.6 = f32[9216,2,3]{2,1,0:T(2,128)} fusion(f32[2,3,4096]{1,0,2:T(2,128)} %bitcast.553, s32[9216]{0:T(1024)S(1)} %maximum_clamp_fusion), kind=kCustom, calls=%fused_computation.3.clone | custom fusion | bytes 479232 | tf_op jit(solution)/shard_map/jit(_take)/gather | solution.py:109
  837.6 42.6 %fusion = f32[2,1,3,9216]{2,0,3,1:T(2,128)S(1)} fusion(f32[9216,2,3]{2,1,0:T(2,128)} %gather_fusion.6, pred[9216]{0:T(1024)(128)(4,1)S(1)} %get-tuple-element.38, pred[9216]{0:T(1024)(128)(4,1)S(1)} %get-tuple-element.37), kind=kLoop, calls=%fused_computation.9 | loop fusion | flops 110592 | bytes 460800 | tf_op jit(solution)/shard_map/jit(_where)/select_n | solution.py:110
  880.2 8.5 fusion.514
  888.7 3.1 copy.293
  892.8 3.1 copy.294
  899.9 59.6 %all-reduce.2.cloned.1.call-done = f32[3,9216]{1,0:T(4,128)} async-done(((f32[3,9216]{1,0:T(4,128)}), f32[3,9216]{1,0:T(4,128)}) %all-reduce.2.cloned.1.call-update) | async-done | bytes 110608 | tf_op jit(solution)/shard_map/psum | solution.py:154
  959.6 1.6 fusion.39
  (169 shorter events, 57.4 us)
Async XLA Ops:
  12.2 104.2 %all-to-all-start = ((f32[2,1,3,32,128]{4,0,2,1,3:T(2,128)}), f32[2,1,3,32,128]{4,0,2,1,3:T(2,128)S(1)}, u32[]{:S(2)}, u32[]{:S(2)}) async-start(f32[2,1,3,32,128]{4,0,2,1,3:T(2,128)} %copy.177), calls=%async_computation | async-start | bytes 196608 | tf_op jit(solution)/shard_map/all_to_all | solution.py:138
  236.8 11.4 %copy-start = (f32[3,9216]{1,0:T(4,128)S(1)}, f32[3,9216]{1,0:T(4,128)}, u32[]{:S(2)}) copy-start(f32[3,9216]{1,0:T(4,128)} %param.7) | copy-start | bytes 331780
  249.7 57.6 %copy-start.3 = (s32[128]{0:T(128)S(1)}, s32[128]{0:T(128)}, u32[]{:S(2)}) copy-start(s32[128]{0:T(128)} %param.9) | copy-start | bytes 1540
  252.4 66.7 %copy-start.1 = (f32[2,1,128,128]{3,2,1,0:T(8,128)S(1)}, f32[2,1,128,128]{3,2,1,0:T(8,128)}, u32[]{:S(2)}) copy-start(f32[2,1,128,128]{3,2,1,0:T(8,128)} %param.6) | copy-start | bytes 393220
  300.9 15.3 %all-to-all-start.1 = ((f32[2,1,3,32,128]{4,0,2,1,3:T(2,128)}), f32[2,1,3,32,128]{4,0,2,1,3:T(2,128)S(1)}, u32[]{:S(2)}, u32[]{:S(2)}) async-start(f32[2,1,3,32,128]{4,0,2,1,3:T(2,128)} %copy.196), calls=%async_computation.1 | async-start | bytes 196608 | tf_op jit(solution)/shard_map/all_to_all | solution.py:146
  518.8 14.4 %all-to-all-start.3 = ((f32[2,1,3,32,128]{4,0,2,1,3:T(2,128)}), f32[2,1,3,32,128]{4,0,2,1,3:T(2,128)S(1)}, u32[]{:S(2)}, u32[]{:S(2)}) async-start(f32[2,1,3,32,128]{4,0,2,1,3:T(2,128)} %copy.218), calls=%async_computation.3 | async-start | bytes 196608 | tf_op jit(solution)/shard_map/all_to_all | solution.py:146
  735.8 14.0 %all-to-all-start.5 = ((f32[2,1,3,32,128]{4,0,2,1,3:T(2,128)}), f32[2,1,3,32,128]{4,0,2,1,3:T(2,128)S(1)}, u32[]{:S(2)}, u32[]{:S(2)}) async-start(f32[2,1,3,32,128]{4,0,2,1,3:T(2,128)} %copy.240), calls=%async_computation.5 | async-start | bytes 196608 | tf_op jit(solution)/shard_map/all_to_all | solution.py:146
  740.7 218.8 %all-reduce.2.cloned.1.call-start = ((), (), s32[]{:S(2)}) async-start(), calls=%async_computation.7 | async-start | bytes 294912 | tf_op jit(solution)/shard_map/psum | solution.py:154
  752.7 127.4 %copy-start.2 = (f32[2,1,128,128]{3,2,1,0:T(8,128)}, f32[2,1,128,128]{3,2,1,0:T(8,128)S(1)}, u32[]{:S(2)}) copy-start(f32[2,1,128,128]{3,2,1,0:T(8,128)S(1)} %maximum_add_fusion.3) | copy-start | bytes 393220
Sparse Core Ops, SparseCore 0:
  900.1 59.4 all-reduce.1
where the time goes:
time: 975 us; the launch traced here: 968 us
  local copies, waits for them, and re-layouts  501 us (51%)
  other arithmetic  177 us (18%)
  blocking collectives  117 us (12%)
  waiting for transfers between devices  86.1 us (9%)
  matrix products  43.7 us (4%)
  starting transfers between devices  28.8 us (3%)
  between operations  15.4 us (2%)
    gather x4, local copies, waits for them, and re-layouts, spread_columns(): picked = jnp.take(values, jnp.maximum(table, 0), axis=3)  260 us
    select_n x4, other arithmetic, spread_columns(): return jnp.where(table >= 0, picked, 0.0)  170 us
    gather x3, local copies, waits for them, and re-layouts, shards(): spectrum[:, :, :, columns].reshape(2, bands, planes, device_list, slots)  95.5 us
    psum x1, waiting for transfers between devices, shards(): whole = lax.psum(change, 'band')  59.6 us
    all_gather x1, blocking collectives, shards(): lax.all_gather(stick_length, 'plane', axis=0, tiled=True)  39.6 us
    all_gather x1, blocking collectives, shards(): lax.all_gather(stick_column, 'plane', axis=0, tiled=True)  36.7 us
    slice x7, local copies, waits for them, and re-layouts, plane_transform(): imag_part = values[1].reshape(bands, planes, NG, NG)  35.9 us
    another operation x15, local copies, waits for them, and re-layouts, plane_transform(): jnp.stack([final_real, final_imag]).reshape(2, bands, planes, NG * NG)  29.1 us
  transfers between devices with their start and end apart: 5, of which 4 were waited for; matrix products, arithmetic and copies ran while one was open for 2% of the time, Pallas kernels for 0%

commit v1 on v0

--- a/solution.py
+++ b/solution.py
@@ -151,7 +151,9 @@
     ).reshape(2, bands, planes, device_list * slots)
     after = modulus(plane_transform(spread_columns(arrived, given_cells), cosine, sine))
     change = (after - before) / BAND_DEV
-    whole = lax.psum(change, "band")
+    whole = change
+    for hop in (1, 2, 4):
+        whole = whole + lax.ppermute(whole, "band", [(dev, dev ^ hop) for dev in range(8)])
     potential_new = potential + LINEAR_GAIN * whole + CUBIC_GAIN * whole * whole * whole
     return (total, potential_new)
 

time: 975 us -> 918 us (0.942)
  waiting for transfers between devices: 86.1 us -> 35.7 us
  between operations: 15.4 us -> 2.06 us
    psum x1 -> x0, waiting for transfers between devices: 59.6 us -> none  [shards(): whole = lax.psum(change, 'band')]
  transfers between devices with their start and end apart: 5 -> 7, of which waited for: 4 -> 6; matrix products, arithmetic and copies ran while one was open for 2% -> 2% of each run, Pallas kernels for 0% -> 0%
where the time goes in v1:
time: 918 us; the launch traced here: 911 us
  local copies, waits for them, and re-layouts  503 us (55%)
  other arithmetic  176 us (19%)
  blocking collectives  117 us (13%)
  matrix products  43.7 us (5%)
  waiting for transfers between devices  35.7 us (4%)
  starting transfers between devices  33.9 us (4%)
    gather x4, local copies, waits for them, and re-layouts, spread_columns(): picked = jnp.take(values, jnp.maximum(table, 0), axis=3)  262 us
    select_n x4, other arithmetic, spread_columns(): return jnp.where(table >= 0, picked, 0.0)  170 us
    gather x3, local copies, waits for them, and re-layouts, shards(): spectrum[:, :, :, columns].reshape(2, bands, planes, device_list, slots)  96.2 us
    all_gather x1, blocking collectives, shards(): lax.all_gather(stick_length, 'plane', axis=0, tiled=True)  39.6 us
    all_gather x1, blocking collectives, shards(): lax.all_gather(stick_column, 'plane', axis=0, tiled=True)  36.7 us
    slice x7, local copies, waits for them, and re-layouts, plane_transform(): imag_part = values[1].reshape(bands, planes, NG, NG)  35.9 us
    another operation x15, local copies, waits for them, and re-layouts, plane_transform(): jnp.stack([final_real, final_imag]).reshape(2, bands, planes, NG * NG)  29.1 us
    all_to_all x2, blocking collectives, shards(): lax.all_to_all(along_height(term, own), 'plane', split_axis=3, concat_axi...  27 us
  transfers between devices with their start and end apart: 7, of which 6 were waited for; matrix products, arithmetic and copies ran while one was open for 2% of the time, Pallas kernels for 0%

profile of v1, /device:TPU:2, one launch (start us, length us, event | category | flops | bytes accessed | tf_op | source)
XLA Modules:
  0.0 910.6 jit_solution(17728105255535774309)
XLA Ops:
  5.7 11.6 %all-to-all-start = ((f32[2,1,3,32,128]{4,0,2,1,3:T(2,128)}), f32[2,1,3,32,128]{4,0,2,1,3:T(2,128)S(1)}, u32[]{:S(2)}, u32[]{:S(2)}) async-start(f32[2,1,3,32,128]{4,0,2,1,3:T(2,128)} %copy.177), calls=%async_computation | async-start | bytes 196608 | tf_op jit(solution)/shard_map/all_to_all | solution.py:138
  17.3 39.6 %all-gather = s32[32,1,128]{2,1,0:T(1,128)S(1)} all-gather(s32[1,1,128]{2,1,0:T(1,128)} %bitcast.566), channel_id=1, replica_groups=mesh['band'=8,'plane'=32] {'plane'}, dimensions={0}, use_global_device_ids=true | all-gather | bytes 16896 | tf_op jit(solution)/shard_map/all_gather | solution.py:132
  56.9 36.7 %all-gather.1 = s32[32,1,128]{2,1,0:T(1,128)S(1)} all-gather(s32[1,1,128]{2,1,0:T(1,128)} %bitcast.567), channel_id=1, replica_groups=mesh['band'=8,'plane'=32] {'plane'}, dimensions={0}, use_global_device_ids=true | all-gather | bytes 16896 | tf_op jit(solution)/shard_map/all_gather | solution.py:131
  93.6 15.5 %scatter_custom_fusion = s32[9216]{0:T(1024)S(1)} fusion(s32[4096]{0:T(1024)S(1)} %get-tuple-element.40, s32[4096]{0:T(1024)S(1)} %iota.105, s32[]{:T(128)} %constant.56.clone.1), kind=kCustom, calls=%fused_computation.291 | custom fusion | bytes 36868 | tf_op jit(solution)/shard_map/scatter | solution.py:105
  109.9 4.4 copy.179
  114.2 65.4 %gather_fusion.3 = f32[9216,2,3]{2,1,0:T(2,128)} fusion(f32[2,3,4096]{1,0,2:T(2,128)} %bitcast.554, s32[9216]{0:T(1024)S(1)} %maximum_clamp_fusion), kind=kCustom, calls=%fused_computation.clone | custom fusion | bytes 479232 | tf_op jit(solution)/shard_map/jit(_take)/gather | solution.py:109
  179.6 42.6 %fusion.3 = f32[2,1,3,9216]{2,0,3,1:T(2,128)S(1)} fusion(f32[9216,2,3]{2,1,0:T(2,128)} %gather_fusion.3, pred[9216]{0:T(1024)(128)(4,1)S(1)} %get-tuple-element.38, pred[9216]{0:T(1024)(128)(4,1)S(1)} %get-tuple-element.37), kind=kLoop, calls=%fused_computation.15 | loop fusion | flops 110592 | bytes 460800 | tf_op jit(solution)/shard_map/jit(_where)/select_n | solution.py:110
  222.2 8.5 fusion.517
  230.7 3.1 copy.281
  234.8 3.6 copy.282
  248.2 8.9 copy.194
  257.1 32.1 %gather_fusion = f32[4096,2,3]{2,1,0:T(2,128)} fusion(f32[2,3,9216]{1,0,2:T(2,128)} %bitcast.550, s32[4096]{0:T(1024)S(1)} %get-tuple-element.39), kind=kCustom, calls=%fused_computation.4 | custom fusion | bytes 212992 | tf_op jit(solution)/shard_map/gather | solution.py:145
  289.2 5.8 copy.196
  295.0 6.5 all-to-all-start.1
  301.6 8.7 all-to-all-done.1
  315.3 13.5 %all_to_all.35 = f32[2,1,3,32,128]{4,0,2,1,3:T(2,128)S(1)} all-to-all(f32[2,1,3,32,128]{4,0,2,1,3:T(2,128)S(1)} %copy.199), channel_id=1, replica_groups=mesh['band'=8,'plane'=32] {'plane'}, dimensions={3} | all-to-all | bytes 196608 | tf_op jit(solution)/shard_map/all_to_all | solution.py:138
  328.8 4.4 copy.201
  333.1 65.4 %gather_fusion.4 = f32[9216,2,3]{2,1,0:T(2,128)} fusion(f32[2,3,4096]{1,0,2:T(2,128)} %bitcast.555, s32[9216]{0:T(1024)S(1)} %maximum_clamp_fusion), kind=kCustom, calls=%fused_computation.1.clone | custom fusion | bytes 479232 | tf_op jit(solution)/shard_map/jit(_take)/gather | solution.py:109
  398.5 42.6 %fusion.2 = f32[2,1,3,9216]{2,0,3,1:T(2,128)S(1)} fusion(f32[9216,2,3]{2,1,0:T(2,128)} %gather_fusion.4, pred[9216]{0:T(1024)(128)(4,1)S(1)} %get-tuple-element.38, pred[9216]{0:T(1024)(128)(4,1)S(1)} %get-tuple-element.37), kind=kLoop, calls=%fused_computation.13 | loop fusion | flops 110592 | bytes 460800 | tf_op jit(solution)/shard_map/jit(_where)/select_n | solution.py:110
  441.1 8.5 fusion.516
  449.6 3.1 copy.285
  453.7 3.3 copy.286
  466.8 8.9 copy.216
  475.7 32.1 %gather_fusion.1 = f32[4096,2,3]{2,1,0:T(2,128)} fusion(f32[2,3,9216]{1,0,2:T(2,128)} %bitcast.552, s32[4096]{0:T(1024)S(1)} %get-tuple-element.39), kind=kCustom, calls=%fused_computation.5 | custom fusion | bytes 212992 | tf_op jit(solution)/shard_map/gather | solution.py:145
  507.8 5.8 copy.218
  513.6 5.5 all-to-all-start.3
  519.1 8.9 all-to-all-done.3
  532.9 13.5 %all_to_all.36 = f32[2,1,3,32,128]{4,0,2,1,3:T(2,128)S(1)} all-to-all(f32[2,1,3,32,128]{4,0,2,1,3:T(2,128)S(1)} %copy.221), channel_id=1, replica_groups=mesh['band'=8,'plane'=32] {'plane'}, dimensions={3} | all-to-all | bytes 196608 | tf_op jit(solution)/shard_map/all_to_all | solution.py:138
  546.4 4.4 copy.223
  550.8 65.4 %gather_fusion.5 = f32[9216,2,3]{2,1,0:T(2,128)} fusion(f32[2,3,4096]{1,0,2:T(2,128)} %bitcast.556, s32[9216]{0:T(1024)S(1)} %maximum_clamp_fusion), kind=kCustom, calls=%fused_computation.2.clone | custom fusion | bytes 479232 | tf_op jit(solution)/shard_map/jit(_take)/gather | solution.py:109
  616.2 42.6 %fusion.1 = f32[2,1,3,9216]{2,0,3,1:T(2,128)S(1)} fusion(f32[9216,2,3]{2,1,0:T(2,128)} %gather_fusion.5, pred[9216]{0:T(1024)(128)(4,1)S(1)} %get-tuple-element.38, pred[9216]{0:T(1024)(128)(4,1)S(1)} %get-tuple-element.37), kind=kLoop, calls=%fused_computation.11 | loop fusion | flops 110592 | bytes 460800 | tf_op jit(solution)/shard_map/jit(_where)/select_n | solution.py:110
  658.7 8.5 fusion.515
  667.2 3.1 copy.289
  671.3 3.3 copy.290
  684.4 8.9 copy.238
  693.3 32.1 %gather_fusion.2 = f32[4096,2,3]{2,1,0:T(2,128)} fusion(f32[2,3,9216]{1,0,2:T(2,128)} %bitcast.551, s32[4096]{0:T(1024)S(1)} %get-tuple-element.39), kind=kCustom, calls=%fused_computation.6 | custom fusion | bytes 212992 | tf_op jit(solution)/shard_map/gather | solution.py:145
  725.4 5.8 copy.240
  731.2 5.3 all-to-all-start.5
  736.5 8.9 all-to-all-done.5
  750.4 13.5 %all_to_all.37 = f32[2,1,3,32,128]{4,0,2,1,3:T(2,128)S(1)} all-to-all(f32[2,1,3,32,128]{4,0,2,1,3:T(2,128)S(1)} %copy.243), channel_id=1, replica_groups=mesh['band'=8,'plane'=32] {'plane'}, dimensions={3} | all-to-all | bytes 196608 | tf_op jit(solution)/shard_map/all_to_all | solution.py:149
  763.9 4.4 copy.245
  768.3 65.4 %gather_fusion.6 = f32[9216,2,3]{2,1,0:T(2,128)} fusion(f32[2,3,4096]{1,0,2:T(2,128)} %bitcast.553, s32[9216]{0:T(1024)S(1)} %maximum_clamp_fusion), kind=kCustom, calls=%fused_computation.3.clone | custom fusion | bytes 479232 | tf_op jit(solution)/shard_map/jit(_take)/gather | solution.py:109
  833.7 42.6 %fusion = f32[2,1,3,9216]{2,0,3,1:T(2,128)S(1)} fusion(f32[9216,2,3]{2,1,0:T(2,128)} %gather_fusion.6, pred[9216]{0:T(1024)(128)(4,1)S(1)} %get-tuple-element.38, pred[9216]{0:T(1024)(128)(4,1)S(1)} %get-tuple-element.37), kind=kLoop, calls=%fused_computation.9 | loop fusion | flops 110592 | bytes 460800 | tf_op jit(solution)/shard_map/jit(_where)/select_n | solution.py:110
  876.2 8.5 fusion.514
  888.8 3.1 copy.294
  898.5 4.3 collective-permute-done.1
  902.9 3.3 collective-permute-start.2
  906.2 3.5 collective-permute-done.2
  (174 shorter events, 63.5 us)
Async XLA Ops:
  5.7 104.2 %all-to-all-start = ((f32[2,1,3,32,128]{4,0,2,1,3:T(2,128)}), f32[2,1,3,32,128]{4,0,2,1,3:T(2,128)S(1)}, u32[]{:S(2)}, u32[]{:S(2)}) async-start(f32[2,1,3,32,128]{4,0,2,1,3:T(2,128)} %copy.177), calls=%async_computation | async-start | bytes 196608 | tf_op jit(solution)/shard_map/all_to_all | solution.py:138
  230.7 11.4 %copy-start = (f32[3,9216]{1,0:T(4,128)S(1)}, f32[3,9216]{1,0:T(4,128)}, u32[]{:S(2)}) copy-start(f32[3,9216]{1,0:T(4,128)} %param.7) | copy-start | bytes 331780
  243.6 57.8 %copy-start.3 = (s32[128]{0:T(128)S(1)}, s32[128]{0:T(128)}, u32[]{:S(2)}) copy-start(s32[128]{0:T(128)} %param.9) | copy-start | bytes 1540
  246.3 66.9 %copy-start.1 = (f32[2,1,128,128]{3,2,1,0:T(8,128)S(1)}, f32[2,1,128,128]{3,2,1,0:T(8,128)}, u32[]{:S(2)}) copy-start(f32[2,1,128,128]{3,2,1,0:T(8,128)} %param.6) | copy-start | bytes 393220
  295.0 15.3 %all-to-all-start.1 = ((f32[2,1,3,32,128]{4,0,2,1,3:T(2,128)}), f32[2,1,3,32,128]{4,0,2,1,3:T(2,128)S(1)}, u32[]{:S(2)}, u32[]{:S(2)}) async-start(f32[2,1,3,32,128]{4,0,2,1,3:T(2,128)} %copy.196), calls=%async_computation.1 | async-start | bytes 196608 | tf_op jit(solution)/shard_map/all_to_all | solution.py:146
  513.6 14.4 %all-to-all-start.3 = ((f32[2,1,3,32,128]{4,0,2,1,3:T(2,128)}), f32[2,1,3,32,128]{4,0,2,1,3:T(2,128)S(1)}, u32[]{:S(2)}, u32[]{:S(2)}) async-start(f32[2,1,3,32,128]{4,0,2,1,3:T(2,128)} %copy.218), calls=%async_computation.3 | async-start | bytes 196608 | tf_op jit(solution)/shard_map/all_to_all | solution.py:146
  731.2 14.2 %all-to-all-start.5 = ((f32[2,1,3,32,128]{4,0,2,1,3:T(2,128)}), f32[2,1,3,32,128]{4,0,2,1,3:T(2,128)S(1)}, u32[]{:S(2)}, u32[]{:S(2)}) async-start(f32[2,1,3,32,128]{4,0,2,1,3:T(2,128)} %copy.240), calls=%async_computation.5 | async-start | bytes 196608 | tf_op jit(solution)/shard_map/all_to_all | solution.py:146
  748.4 127.9 %copy-start.2 = (f32[2,1,128,128]{3,2,1,0:T(8,128)}, f32[2,1,128,128]{3,2,1,0:T(8,128)S(1)}, u32[]{:S(2)}) copy-start(f32[2,1,128,128]{3,2,1,0:T(8,128)S(1)} %maximum_add_fusion.3) | copy-start | bytes 393220
  895.3 1.5 collective-permute-start
  896.8 6.0 collective-permute-start.1
  902.9 6.7 collective-permute-start.2
